TPU v7x, 256 devices: a whole 4x4x8 slice. The times are simulated.
256 devices in a mesh: dp: 32 (over y_hi, z, core), fsdp: 8 (over x, y_lo).
Axes of the slice: x: 4, y: 4 (y_hi: 2, y_lo: 2; y = y_hi * 2 + y_lo), z: 8, core: 2. Of those that a mesh axis runs over, the one named last changes fastest.
Arguments:
- tokens: bfloat16 [4096, 4096], P(('fsdp', 'dp')), may hold values from -6 to 6
- upstream: bfloat16 [4096, 4096], P(('fsdp', 'dp')), may hold values from -0.375 to 0.375
- old_master: float32 [4096, 3, 5632], P(('fsdp', 'dp')), may hold values from -0.09375 to 0.09375
- old_first: float32 [4096, 3, 5632], P(('fsdp', 'dp')), may hold values from -3 to 3
- old_second: float32 [4096, 3, 5632], P(('fsdp', 'dp')), may hold values from 0.01 to 4
- grown_master: float32 [4096, 3, 2560], P(('fsdp', 'dp')), may hold values from -0.09375 to 0.09375
- grown_first: float32 [4096, 3, 2560], P(('fsdp', 'dp')), may hold values from -3 to 3
- grown_second: float32 [4096, 3, 2560], P(('fsdp', 'dp')), may hold values from 0.01 to 4
- grow_mask: float32 [2560], replicated, may hold values from 0.1 to 1
Outputs:
- layer_output: bfloat16 [4096, 4096], P(('fsdp', 'dp'))
- new_master: float32 [4096, 3, 8192], P('fsdp', None, 'dp')
- new_first: float32 [4096, 3, 8192], P('fsdp', None, 'dp')
- new_second: float32 [4096, 3, 8192], P('fsdp', None, 'dp')
All inputs are finite; a program needn't handle non-finite values.
Results may differ from a plain program's by a relative error of at most 0.019.
Values may be sent and summed in bfloat16 or wider, within the bound.
A program may use at most 128 MiB of HBM per device.

v0:
```python
import jax
import jax.numpy as jnp
from jax import lax
from jax.sharding import PartitionSpec as P

STEP = 1000
beta_first = 0.9
beta_second = 0.999
adam_epsilon = 1e-08
learn_rate = 0.001
weight_decay = 0.1


def sent_together(arrays, axis, dim, along):
    both = jnp.concatenate(arrays, axis=along)
    filled, at, gathered = (lax.all_gather(both, axis, axis=dim, tiled=True), 0, [])
    for a in arrays:
        gathered.append(lax.slice_in_dim(filled, at, at + a.shape[along], axis=along))
        at += a.shape[along]
    return tuple(gathered)


def split_up(array, dim, size):
    lengths = array.shape
    parts = array.reshape(*lengths[:dim], size, lengths[dim] // size, *lengths[dim + 1 :])
    return jnp.moveaxis(parts, dim, 0)


def sent_and_summed(array, axis, dim):
    parts = split_up(array, dim, lax.axis_size(axis))
    arrived = lax.all_to_all(parts, axis, split_axis=0, concat_axis=0, tiled=True)
    return arrived.astype(jnp.float32).sum(axis=0)


def in_one_piece(arrays, axis, split_dim, concat_dim, along):
    both = jnp.concatenate(arrays, axis=along)
    filled, at, gathered = (
        lax.all_to_all(both, axis, split_axis=split_dim, concat_axis=concat_dim, tiled=True),
        0,
        [],
    )
    for a in arrays:
        gathered.append(lax.slice_in_dim(filled, at, at + a.shape[along], axis=along))
        at += a.shape[along]
    return tuple(gathered)


def contract_rows(left_part, right_part):
    return lax.dot_general(
        left_part, right_part, (((0,), (0,)), ((), ())), preferred_element_type=jnp.float32
    )


def contract_last(left_part, right_part):
    return lax.dot_general(
        left_part, right_part, (((1,), (1,)), ((), ())), preferred_element_type=jnp.float32
    )


def adam_update(master, first_moment, second_moment, gradients):
    new_first = beta_first * first_moment + (1.0 - beta_first) * gradients
    new_second = beta_second * second_moment + (1.0 - beta_second) * gradients * gradients
    first_hat = new_first / (1.0 - beta_first**STEP)
    second_hat = new_second / (1.0 - beta_second**STEP)
    new_master = master - learn_rate * (
        first_hat / (jnp.sqrt(second_hat) + adam_epsilon) + weight_decay * master
    )
    return (new_master, new_first, new_second)


def local(
    tokens,
    upstream,
    old_master,
    old_first,
    old_second,
    grown_master,
    grown_first,
    grown_second,
    grow_mask,
):
    new_width = old_master.shape[2] + grown_master.shape[2]
    block_width = new_width // lax.axis_size("dp")
    master_all = jnp.concatenate([old_master, grown_master], axis=2)
    first_all = jnp.concatenate([old_first, grown_first], axis=2)
    second_all = jnp.concatenate([old_second, grown_second], axis=2)
    master = lax.all_to_all(
        master_all.astype(jnp.bfloat16), "dp", split_axis=2, concat_axis=0, tiled=True
    ).astype(master_all.dtype)
    weights = lax.all_gather(master.astype(jnp.bfloat16), "fsdp", axis=0, tiled=True)
    rows_in, rows_back = sent_together((tokens, upstream), "dp", 0, 1)
    all_scales = jnp.concatenate([jnp.ones((old_master.shape[2],), jnp.float32), grow_mask])
    scales = lax.dynamic_slice_in_dim(all_scales, lax.axis_index("dp") * block_width, block_width)
    model_width = weights.shape[0]
    paired = weights[:, :2, :].reshape(model_width, 2 * block_width)
    down_weights = weights[:, 2, :]
    projected = jnp.dot(rows_in, paired, preferred_element_type=jnp.float32)
    gate_value = projected[:, :block_width]
    up_value = projected[:, block_width:]
    sigmoid_gate = jax.nn.sigmoid(gate_value)
    activated = gate_value * sigmoid_gate
    hidden = (activated * up_value * scales).astype(jnp.bfloat16)
    summed = lax.psum_scatter(
        contract_last(hidden, down_weights).astype(jnp.bfloat16),
        "dp",
        scatter_dimension=0,
        tiled=True,
    )
    back_hidden = jnp.dot(rows_back, down_weights, preferred_element_type=jnp.float32) * scales
    own_rows = master.shape[0]
    down_grad = sent_and_summed(contract_rows(rows_back, hidden).astype(jnp.bfloat16), "fsdp", 0)
    gate_back = (
        back_hidden * up_value * sigmoid_gate * (1.0 + gate_value * (1.0 - sigmoid_gate))
    ).astype(jnp.bfloat16)
    up_back = (back_hidden * activated).astype(jnp.bfloat16)
    inner_back = jnp.concatenate([gate_back, up_back], axis=1)
    inner_grad = sent_and_summed(contract_rows(rows_in, inner_back).astype(jnp.bfloat16), "fsdp", 0)
    gradients = jnp.concatenate(
        [inner_grad.reshape(own_rows, 2, block_width), down_grad[:, None, :]], axis=1
    )
    first_moment, second_moment = tuple(
        (
            part.astype(jnp.float32)
            for part in in_one_piece(
                (first_all.astype(jnp.bfloat16), second_all.astype(jnp.bfloat16)), "dp", 2, 0, 1
            )
        )
    )
    new_master, new_first, new_second = adam_update(master, first_moment, second_moment, gradients)
    return (summed, new_master, new_first, new_second)


def solution(mesh):
    in_specs = (
        P(("fsdp", "dp"), None),
        P(("fsdp", "dp"), None),
        P(("fsdp", "dp"), None, None),
        P(("fsdp", "dp"), None, None),
        P(("fsdp", "dp"), None, None),
        P(("fsdp", "dp"), None, None),
        P(("fsdp", "dp"), None, None),
        P(("fsdp", "dp"), None, None),
        P(),
    )
    out_specs = (
        P(("fsdp", "dp"), None),
        P("fsdp", None, "dp"),
        P("fsdp", None, "dp"),
        P("fsdp", None, "dp"),
    )
    return jax.shard_map(local, mesh=mesh, in_specs=in_specs, out_specs=out_specs, check_vma=False)
```

profile of v0, /device:TPU:4, one launch (start us, length us, event | category | flops | bytes accessed | tf_op | source)
XLA Modules:
  0.0 517.3 jit_solution(11075435288912256371)
XLA Ops:
  7.2 0.0 all-gather.5.cloned.1.call-start
  7.2 1.1 convert.19
  8.3 1.3 convert.18
  9.6 0.1 pad_maximum_fusion.1
  9.6 8.3 %copy.39 = bf16[16,3,8192]{0,1,2:T(4,128)(2,1)} copy(bf16[16,3,8192]{2,0,1:T(8,128)(2,1)S(1)} %pad_maximum_fusion.1) | data formatting | bytes 1572864 | tf_op jit(solution)/shard_map/concatenate | solution.py:84
  17.9 12.8 %reshape.25 = bf16[32,2,6144]{2,1,0:T(2,128)(2,1)S(1)} reshape(bf16[8192,3,16]{2,1,0:T(4,128)(2,1)} %bitcast.33) | data formatting | bytes 1572864
  30.7 36.1 %all_to_all.46 = bf16[32,2,6144]{2,1,0:T(2,128)(2,1)S(1)} all-to-all(bf16[32,2,6144]{2,1,0:T(2,128)(2,1)S(1)} %reshape.25), channel_id=1, replica_groups=mesh['dp'=32,'fsdp'=8] {'dp'}, dimensions={0} | all-to-all | bytes 1572864 | tf_op jit(solution)/shard_map/all_to_all | solution.py:87
  66.8 10.7 %reshape.26 = bf16[8192,3,16]{2,1,0:T(4,128)(2,1)} reshape(bf16[32,2,6144]{2,1,0:T(2,128)(2,1)S(1)} %all_to_all.46) | data formatting | bytes 1572864
  77.5 10.9 %copy.49 = bf16[16,3,32,256]{3,0,2,1:T(8,128)(2,1)} copy(bf16[16,3,32,256]{0,1,3,2:T(4,128)(2,1)} %bitcast.34) | data formatting | bytes 1572864 | tf_op jit(solution)/shard_map/all_to_all | solution.py:87
  88.5 0.0 all-gather.5.cloned.1.call-update
  88.5 0.0 copy-start.4
  88.5 0.0 all-gather.3.cloned.1.call-start
  88.6 0.7 pad_maximum_fusion.2
  89.3 0.0 all-gather.3.cloned.1.call-update
  89.4 0.4 copy-done.3
  89.8 0.1 convert.22
  89.8 0.1 copy-done.6
  89.9 0.3 copy-done.4
  90.3 0.1 convert.20
  90.3 0.1 maximum_maximum_fusion
  90.5 13.0 %copy.43 = bf16[16,6,8192]{0,1,2:T(8,128)(2,1)} copy(bf16[16,6,8192]{2,0,1:T(8,128)(2,1)S(1)} %maximum_maximum_fusion) | data formatting | bytes 3145728 | tf_op jit(solution)/shard_map/concatenate | solution.py:36
  103.5 18.7 %reshape.27 = bf16[32,2,12288]{2,1,0:T(2,128)(2,1)} reshape(bf16[8192,6,16]{2,1,0:T(8,128)(2,1)} %bitcast.31) | data formatting | bytes 3145728
  122.2 4.1 all-to-all-start.1
  126.4 0.1 pad_dynamic-slice_fusion
  126.4 105.6 %all-gather.5.cloned.1.call-done = bf16[4096,3,256]{2,0,1:T(8,128)(2,1)} async-done(((bf16[512,3,256]{2,0,1:T(8,128)(2,1)}), bf16[4096,3,256]{2,0,1:T(8,128)(2,1)}) %all-gather.5.cloned.1.call-update) | async-done | bytes 6291472 | tf_op jit(solution)/shard_map/all_gather | solution.py:90
  232.1 4.4 slice.33
  236.5 6.5 %copy.42 = bf16[4096,2,256]{0,2,1:T(8,128)(2,1)} copy(bf16[4096,2,256]{2,0,1:T(8,128)(2,1)} %slice.33) | data formatting | bytes 8388608 | tf_op jit(solution)/shard_map/slice | solution.py:95
  243.0 95.1 %all-gather.3.cloned.1.call-done = bf16[512,8192]{1,0:T(8,128)(2,1)} async-done(((bf16[16,8192]{1,0:T(8,128)(2,1)}), bf16[512,8192]{1,0:T(8,128)(2,1)}) %all-gather.3.cloned.1.call-update) | async-done | bytes 8388624 | tf_op jit(solution)/shard_map/all_gather | solution.py:16
  338.1 6.0 %fusion.4 = f32[512,512]{0,1:T(8,128)S(1)} fusion(bf16[4096,512]{0,1:T(8,128)(2,1)} %bitcast.38, bf16[512,8192]{1,0:T(8,128)(2,1)} %all-gather.3.cloned.1.call-done), kind=kOutput, calls=%fused_computation.9 | convolution fusion | flops 2147483648 | bytes 9437184 | tf_op jit(solution)/shard_map/dot_general | solution.py:97
  344.0 3.1 multiply_convert_fusion.1
  347.2 2.7 convolution_convert_fusion.2
  349.8 1.1 copy-done.1
  351.0 4.8 all-to-all-start.3
  355.8 4.8 convolution_convert_fusion
  360.6 0.0 reduce-scatter.2.cloned.1.call-update
  360.7 6.6 %convolution_convert_fusion.1 = bf16[4096,512]{1,0:T(8,128)(2,1)} fusion(bf16[512,8192]{1,0:T(8,128)(2,1)} %all-gather.3.cloned.1.call-done, bf16[512,256]{0,1:T(8,128)(2,1)S(1)} %get-tuple-element.12, bf16[512,256]{0,1:T(8,128)(2,1)S(1)} %get-tuple-element.11), kind=kOutput, calls=%fused_computation.2 | convolution fusion | flops 2150629376 | bytes 8912896 | tf_op jit(solution)/shard_map/dot_general | solution.py:49
  367.2 16.5 %all-to-all-done.3 = bf16[8,512,256]{2,1,0:T(8,128)(2,1)S(1)} async-done(((bf16[8,512,256]{2,1,0:T(8,128)(2,1)}), bf16[8,512,256]{2,1,0:T(8,128)(2,1)S(1)}, u32[]{:S(2)}, u32[]{:S(2)}) %all-to-all-start.3) | async-done | bytes 2097184 | tf_op jit(solution)/shard_map/all_to_all | solution.py:31
  383.7 8.4 %all-to-all-start.2 = ((bf16[8,512,512]{2,1,0:T(8,128)(2,1)}), bf16[8,512,512]{2,1,0:T(8,128)(2,1)}, u32[]{:S(2)}, u32[]{:S(2)}) async-start(bf16[8,512,512]{2,1,0:T(8,128)(2,1)} %bitcast.37), calls=%async_computation.3 | async-start | bytes 8388608 | tf_op jit(solution)/shard_map/all_to_all | solution.py:31
  392.1 18.0 %reshape.28 = bf16[8192,6,16]{2,1,0:T(8,128)(2,1)} reshape(bf16[32,2,12288]{2,1,0:T(2,128)(2,1)} %copy-done.1) | data formatting | bytes 3145728
  410.1 15.1 %copy.45 = bf16[32,16,6,256]{3,1,0,2:T(8,128)(2,1)} copy(bf16[32,16,6,256]{1,2,3,0:T(8,128)(2,1)} %bitcast.32) | data formatting | bytes 3145728 | tf_op jit(solution)/shard_map/all_to_all | solution.py:38
  425.2 1.1 convert_reduce_fusion.1
  426.3 21.5 %all-to-all-done.2 = bf16[8,512,512]{2,1,0:T(8,128)(2,1)} async-done(((bf16[8,512,512]{2,1,0:T(8,128)(2,1)}), bf16[8,512,512]{2,1,0:T(8,128)(2,1)}, u32[]{:S(2)}, u32[]{:S(2)}) %all-to-all-start.2) | async-done | bytes 4194336 | tf_op jit(solution)/shard_map/all_to_all | solution.py:31
  447.8 2.9 convert_reduce_fusion
  450.7 0.0 copy-start
  450.7 1.3 copy.46
  452.0 1.6 copy.47
  453.6 4.0 convert_subtract_fusion
  457.6 53.1 %reduce-scatter.2.cloned.1.call-done = bf16[16,4096]{1,0:T(8,128)(2,1)} async-done(((bf16[512,4096]{1,0:T(8,128)(2,1)}), bf16[16,4096]{1,0:T(8,128)(2,1)}) %reduce-scatter.2.cloned.1.call-update) | async-done | bytes 131088 | tf_op jit(solution)/shard_map/reduce_scatter | solution.py:103
  (20 shorter events, 0.1 us)
Async XLA Ops:
  7.2 224.9 %all-gather.5.cloned.1.call-start = ((), (), s32[]{:S(2)}) async-start(), calls=%async_computation.6 | async-start | bytes 7077888 | tf_op jit(solution)/shard_map/all_gather | solution.py:90
  77.5 11.0 %copy-start.7 = (bf16[16,4096]{1,0:T(8,128)(2,1)S(1)}, bf16[16,4096]{1,0:T(8,128)(2,1)}, u32[]{:S(2)}) copy-start(bf16[16,4096]{1,0:T(8,128)(2,1)} %param.10) | copy-start | bytes 393220
  77.5 11.0 %copy-start.8 = (bf16[16,4096]{1,0:T(8,128)(2,1)S(1)}, bf16[16,4096]{1,0:T(8,128)(2,1)}, u32[]{:S(2)}) copy-start(bf16[16,4096]{1,0:T(8,128)(2,1)} %param.9) | copy-start | bytes 393220
  77.5 11.8 %copy-start.5 = (f32[16,3,2560]{2,0,1:T(8,128)S(1)}, f32[16,3,2560]{2,0,1:T(8,128)}, u32[]{:S(2)}) copy-start(f32[16,3,2560]{2,0,1:T(8,128)} %param.16) | copy-start | bytes 1474564
  88.5 1.3 copy-start.3
  88.5 1.4 copy-start.6
  88.5 1.8 copy-start.4
  88.5 249.6 %all-gather.3.cloned.1.call-start = ((), (), s32[]{:S(2)}) async-start(), calls=%async_computation.5 | async-start | bytes 8650752 | tf_op jit(solution)/shard_map/all_gather | solution.py:16
  122.2 4.1 copy-start.9
  122.2 227.6 %all-to-all-start.1 = ((bf16[32,2,12288]{2,1,0:T(2,128)(2,1)}), bf16[32,2,12288]{2,1,0:T(2,128)(2,1)S(1)}, u32[]{:S(2)}, u32[]{:S(2)}) async-start(bf16[32,2,12288]{2,1,0:T(2,128)(2,1)} %reshape.27), calls=%async_computation.2 | async-start | bytes 3145728 | tf_op jit(solution)/shard_map/all_to_all | solution.py:38
  338.1 6.0 %copy-start.10 = (bf16[512,8192]{1,0:T(8,128)(2,1)S(1)}, bf16[512,8192]{1,0:T(8,128)(2,1)}, u32[]{:S(2)}) copy-start(bf16[512,8192]{1,0:T(8,128)(2,1)} %all-gather.3.cloned.1.call-done) | copy-start | bytes 25165828
  349.8 1.1 copy-start.1
  351.0 32.8 %all-to-all-start.3 = ((bf16[8,512,256]{2,1,0:T(8,128)(2,1)}), bf16[8,512,256]{2,1,0:T(8,128)(2,1)S(1)}, u32[]{:S(2)}, u32[]{:S(2)}) async-start(bf16[8,512,256]{2,1,0:T(8,128)(2,1)} %bitcast.41), calls=%async_computation.4 | async-start | bytes 4194304 | tf_op jit(solution)/shard_map/all_to_all | solution.py:31
  355.8 155.0 %reduce-scatter.2.cloned.1.call-start = ((), (), s32[]{:S(2)}) async-start(), calls=%async_computation.7 | async-start | bytes 4325376 | tf_op jit(solution)/shard_map/reduce_scatter | solution.py:103
  383.7 64.0 %all-to-all-start.2 = ((bf16[8,512,512]{2,1,0:T(8,128)(2,1)}), bf16[8,512,512]{2,1,0:T(8,128)(2,1)}, u32[]{:S(2)}, u32[]{:S(2)}) async-start(bf16[8,512,512]{2,1,0:T(8,128)(2,1)} %bitcast.37), calls=%async_computation.3 | async-start | bytes 8388608 | tf_op jit(solution)/shard_map/all_to_all | solution.py:31
  450.7 2.9 copy-start
  450.7 2.9 copy-start.2
Sparse Core Ops, SparseCore 0:
  88.6 143.4 all-gather.4
  235.4 102.5 all-gather.2
  361.4 149.3 reduce-scatter.1
where the time goes:
time: 520 us; the launch traced here: 517 us
  waiting for transfers between devices  292 us (56%)
  local copies, waits for them, and re-layouts  123 us (24%)
  blocking collectives  36.1 us (7%)
  matrix products  23.1 us (4%)
  starting transfers between devices  17.4 us (3%)
  between operations  13.9 us (3%)
  other arithmetic  11.5 us (2%)
    all_gather x1, waiting for transfers between devices, local(): lax.all_gather(master.astype(jnp.bfloat16), 'fsdp', axis=0, tiled=True)  106 us
    all_gather x1, waiting for transfers between devices, sent_together(): lax.all_gather(both, axis, axis=dim, tiled=True)  95.1 us
    unnamed x26, local copies, waits for them, and re-layouts  62.3 us
    reduce_scatter x1, waiting for transfers between devices, local(): lax.psum_scatter(contract_last(hidden, down_weights).astype(jnp.bfloat16)...  53.1 us
    all_to_all x2, waiting for transfers between devices, sent_and_summed(): lax.all_to_all(parts, axis, split_axis=0, concat_axis=0, tiled=True)  38 us
    all_to_all x1, blocking collectives, local(): lax.all_to_all(master_all.astype(jnp.bfloat16), 'dp', split_axis=2, conca...  36.1 us
    all_to_all x1, local copies, waits for them, and re-layouts, in_one_piece(): lax.all_to_all(both, axis, split_axis=split_dim, concat_axis=concat_dim,...  15.1 us
    all_to_all x2, starting transfers between devices, sent_and_summed(): lax.all_to_all(parts, axis, split_axis=0, concat_axis=0, tiled=True)  13.2 us
  transfers between devices with their start and end apart: 6, of which 5 were waited for; matrix products, arithmetic and copies ran while one was open for 21% of the time, Pallas kernels for 0%

commit v1 on v0

--- a/solution.py
+++ b/solution.py
@@ -87,7 +87,12 @@
     master = lax.all_to_all(
         master_all.astype(jnp.bfloat16), "dp", split_axis=2, concat_axis=0, tiled=True
     ).astype(master_all.dtype)
-    weights = lax.all_gather(master.astype(jnp.bfloat16), "fsdp", axis=0, tiled=True)
+    weights = jnp.concatenate(
+        lax.all_to_all(
+            jnp.stack([master.astype(jnp.bfloat16)] * lax.axis_size("fsdp")), "fsdp", 0, 0
+        ),
+        axis=0,
+    )
     rows_in, rows_back = sent_together((tokens, upstream), "dp", 0, 1)
     all_scales = jnp.concatenate([jnp.ones((old_master.shape[2],), jnp.float32), grow_mask])
     scales = lax.dynamic_slice_in_dim(all_scales, lax.axis_index("dp") * block_width, block_width)

time: 520 us -> 401 us (0.77)
  waiting for transfers between devices: 292 us -> 156 us
  starting transfers between devices: 17.4 us -> 27.3 us
    all_gather x1 -> x0, waiting for transfers between devices: 106 us -> none  [local(): lax.all_gather(master.astype(jnp.bfloat16), 'fsdp', axis=0, tiled=True)]
    all_gather x1, waiting for transfers between devices: 95.1 us -> 0.01 us  [sent_together(): lax.all_gather(both, axis, axis=dim, tiled=True)]
    all_to_all x0 -> x1, waiting for transfers between devices: none -> 50 us  [local(): lax.all_to_all(jnp.stack([master.astype(jnp.bfloat16)] * lax.axis_size('f...]
    all_to_all x1, waiting for transfers between devices: 0.01 us -> 19.4 us  [in_one_piece(): lax.all_to_all(both, axis, split_axis=split_dim, concat_axis=concat_dim,...]
    slice x2 -> x1, local copies, waits for them, and re-layouts: 10.9 us -> 2.32 us  [local(): paired = weights[:, :2, :].reshape(model_width, 2 * block_width)]
    all_to_all x0 -> x1, starting transfers between devices: none -> 5.42 us  [local(): lax.all_to_all(jnp.stack([master.astype(jnp.bfloat16)] * lax.axis_size('f...]
  transfers between devices with their start and end apart: 6 -> 6, of which waited for: 5 -> 5; matrix products, arithmetic and copies ran while one was open for 21% -> 39% of each run, Pallas kernels for 0% -> 0%
where the time goes in v1:
time: 401 us; the launch traced here: 399 us
  waiting for transfers between devices  156 us (39%)
  local copies, waits for them, and re-layouts  128 us (32%)
  blocking collectives  37.7 us (9%)
  starting transfers between devices  27.3 us (7%)
  matrix products  23.7 us (6%)
  between operations  14.2 us (4%)
  other arithmetic  11.6 us (3%)
    unnamed x26, local copies, waits for them, and re-layouts  66.5 us
    all_to_all x1, waiting for transfers between devices, local(): lax.all_to_all(jnp.stack([master.astype(jnp.bfloat16)] * lax.axis_size('f...  50 us
    reduce_scatter x1, waiting for transfers between devices, local(): lax.psum_scatter(contract_last(hidden, down_weights).astype(jnp.bfloat16)...  49.8 us
    all_to_all x1, blocking collectives, local(): lax.all_to_all(master_all.astype(jnp.bfloat16), 'dp', split_axis=2, conca...  37.7 us
    all_to_all x2, waiting for transfers between devices, sent_and_summed(): lax.all_to_all(parts, axis, split_axis=0, concat_axis=0, tiled=True)  36.7 us
    all_to_all x1, waiting for transfers between devices, in_one_piece(): lax.all_to_all(both, axis, split_axis=split_dim, concat_axis=concat_dim,...  19.4 us
    all_to_all x2, starting transfers between devices, sent_and_summed(): lax.all_to_all(parts, axis, split_axis=0, concat_axis=0, tiled=True)  15.9 us
    all_to_all x1, local copies, waits for them, and re-layouts, in_one_piece(): lax.all_to_all(both, axis, split_axis=split_dim, concat_axis=concat_dim,...  15.2 us
  transfers between devices with their start and end apart: 6, of which 5 were waited for; matrix products, arithmetic and copies ran while one was open for 39% of the time, Pallas kernels for 0%

profile of v1, /device:TPU:4, one launch (start us, length us, event | category | flops | bytes accessed | tf_op | source)
XLA Modules:
  0.0 398.5 jit_solution(1494171777432167430)
XLA Ops:
  7.2 0.0 all-gather.2.cloned.1.call-start
  7.2 1.8 pad_maximum_fusion.2
  9.0 0.0 all-gather.2.cloned.1.call-update
  9.0 1.1 convert.19
  10.1 0.1 convert.18
  10.1 0.1 pad_maximum_fusion.1
  10.2 8.3 %copy.45 = bf16[16,3,8192]{0,1,2:T(4,128)(2,1)} copy(bf16[16,3,8192]{2,0,1:T(8,128)(2,1)S(1)} %pad_maximum_fusion.1) | data formatting | bytes 1572864 | tf_op jit(solution)/shard_map/concatenate | solution.py:84
  18.5 12.8 %reshape.32 = bf16[32,2,6144]{2,1,0:T(2,128)(2,1)S(1)} reshape(bf16[8192,3,16]{2,1,0:T(4,128)(2,1)} %bitcast.37) | data formatting | bytes 1572864
  31.3 37.7 %all_to_all.48 = bf16[32,2,6144]{2,1,0:T(2,128)(2,1)S(1)} all-to-all(bf16[32,2,6144]{2,1,0:T(2,128)(2,1)S(1)} %reshape.32), channel_id=1, replica_groups=mesh['dp'=32,'fsdp'=8] {'dp'}, dimensions={0} | all-to-all | bytes 1572864 | tf_op jit(solution)/shard_map/all_to_all | solution.py:87
  69.0 10.8 %reshape.33 = bf16[8192,3,16]{2,1,0:T(4,128)(2,1)} reshape(bf16[32,2,6144]{2,1,0:T(2,128)(2,1)S(1)} %all_to_all.48) | data formatting | bytes 1572864
  79.8 10.0 %copy.57 = bf16[16,3,32,256]{3,0,2,1:T(8,128)(2,1)S(1)} copy(bf16[16,3,32,256]{0,1,3,2:T(4,128)(2,1)} %bitcast.38) | data formatting | bytes 1572864 | tf_op jit(solution)/shard_map/all_to_all | solution.py:87
  89.9 0.3 copy.48
  90.2 3.4 stack.5
  93.6 5.4 %all-to-all-start.1 = ((bf16[8,512,3,256]{1,3,2,0:T(8,128)(2,1)}), bf16[8,512,3,256]{1,3,2,0:T(8,128)(2,1)}, u32[]{:S(2)}, u32[]{:S(2)}) async-start(bf16[8,512,3,256]{1,3,2,0:T(8,128)(2,1)} %stack.5), calls=%async_computation.1 | async-start | bytes 12582912 | tf_op jit(solution)/shard_map/all_to_all | solution.py:91
  99.1 0.1 convert.22
  99.1 0.9 copy-done.7
  100.1 0.3 copy-done.5
  100.4 0.1 convert.20
  100.4 0.1 maximum_maximum_fusion
  100.6 13.1 %copy.51 = bf16[16,6,8192]{0,1,2:T(8,128)(2,1)} copy(bf16[16,6,8192]{2,0,1:T(8,128)(2,1)S(1)} %maximum_maximum_fusion) | data formatting | bytes 3145728 | tf_op jit(solution)/shard_map/concatenate | solution.py:36
  113.7 18.9 %reshape.34 = bf16[32,2,12288]{2,1,0:T(2,128)(2,1)} reshape(bf16[8192,6,16]{2,1,0:T(8,128)(2,1)} %bitcast.35) | data formatting | bytes 3145728
  132.5 50.0 %all-to-all-done.1 = bf16[8,512,3,256]{1,3,2,0:T(8,128)(2,1)} async-done(((bf16[8,512,3,256]{1,3,2,0:T(8,128)(2,1)}), bf16[8,512,3,256]{1,3,2,0:T(8,128)(2,1)}, u32[]{:S(2)}, u32[]{:S(2)}) %all-to-all-start.1) | async-done | bytes 6291488 | tf_op jit(solution)/shard_map/all_to_all | solution.py:91
  182.5 6.0 %all-to-all-start.2 = ((bf16[32,2,12288]{2,1,0:T(2,128)(2,1)}), bf16[32,2,12288]{2,1,0:T(2,128)(2,1)S(1)}, u32[]{:S(2)}, u32[]{:S(2)}) async-start(bf16[32,2,12288]{2,1,0:T(2,128)(2,1)} %reshape.34), calls=%async_computation.3 | async-start | bytes 3145728 | tf_op jit(solution)/shard_map/all_to_all | solution.py:38
  188.5 0.1 pad_dynamic-slice_fusion
  188.6 3.7 copy.60
  192.3 2.7 copy-done
  195.0 2.3 slice.33
  197.3 6.0 %fusion.4 = f32[512,512]{0,1:T(8,128)S(1)} fusion(bf16[4096,512]{0,1:T(8,128)(2,1)} %bitcast.45, bf16[512,8192]{1,0:T(8,128)(2,1)} %all-gather.2.cloned.1.call-done), kind=kOutput, calls=%fused_computation.9 | convolution fusion | flops 2147483648 | bytes 9437184 | tf_op jit(solution)/shard_map/dot_general | solution.py:102
  203.3 3.7 multiply_convert_fusion.1
  207.0 2.7 convolution_convert_fusion.2
  209.7 19.4 %all-to-all-done.2 = bf16[32,2,12288]{2,1,0:T(2,128)(2,1)S(1)} async-done(((bf16[32,2,12288]{2,1,0:T(2,128)(2,1)}), bf16[32,2,12288]{2,1,0:T(2,128)(2,1)S(1)}, u32[]{:S(2)}, u32[]{:S(2)}) %all-to-all-start.2) | async-done | bytes 1572896 | tf_op jit(solution)/shard_map/all_to_all | solution.py:38
  229.1 1.1 copy-done.1
  230.2 7.5 %all-to-all-start.4 = ((bf16[8,512,256]{2,1,0:T(8,128)(2,1)}), bf16[8,512,256]{2,1,0:T(8,128)(2,1)S(1)}, u32[]{:S(2)}, u32[]{:S(2)}) async-start(bf16[8,512,256]{2,1,0:T(8,128)(2,1)} %bitcast.48), calls=%async_computation.5 | async-start | bytes 4194304 | tf_op jit(solution)/shard_map/all_to_all | solution.py:31
  237.7 4.8 %convolution_convert_fusion = bf16[512,4096]{1,0:T(8,128)(2,1)} fusion(bf16[512,256]{0,1:T(8,128)(2,1)S(1)} %get-tuple-element.13, bf16[4096,3,256]{0,2,1:T(8,128)(2,1)} %bitcast.41), kind=kOutput, calls=%fused_computation.1 | convolution fusion | flops 1075838976 | bytes 6553600 | tf_op jit(solution)/shard_map/dot_general | solution.py:55
  242.6 0.0 reduce-scatter.2.cloned.1.call-update
  242.6 0.9 copy-done.10
  243.5 6.5 %convolution_convert_fusion.1 = bf16[4096,512]{1,0:T(8,128)(2,1)} fusion(bf16[512,8192]{1,0:T(8,128)(2,1)} %all-gather.2.cloned.1.call-done, bf16[512,256]{0,1:T(8,128)(2,1)S(1)} %copy-done.10, bf16[512,256]{0,1:T(8,128)(2,1)S(1)} %get-tuple-element.11), kind=kOutput, calls=%fused_computation.2 | convolution fusion | flops 2150629376 | bytes 8912896 | tf_op jit(solution)/shard_map/dot_general | solution.py:49
  250.1 14.7 %all-to-all-done.4 = bf16[8,512,256]{2,1,0:T(8,128)(2,1)S(1)} async-done(((bf16[8,512,256]{2,1,0:T(8,128)(2,1)}), bf16[8,512,256]{2,1,0:T(8,128)(2,1)S(1)}, u32[]{:S(2)}, u32[]{:S(2)}) %all-to-all-start.4) | async-done | bytes 2097184 | tf_op jit(solution)/shard_map/all_to_all | solution.py:31
  264.8 8.4 %all-to-all-start.3 = ((bf16[8,512,512]{2,1,0:T(8,128)(2,1)}), bf16[8,512,512]{2,1,0:T(8,128)(2,1)}, u32[]{:S(2)}, u32[]{:S(2)}) async-start(bf16[8,512,512]{2,1,0:T(8,128)(2,1)} %bitcast.44), calls=%async_computation.4 | async-start | bytes 8388608 | tf_op jit(solution)/shard_map/all_to_all | solution.py:31
  273.1 18.0 %reshape.35 = bf16[8192,6,16]{2,1,0:T(8,128)(2,1)} reshape(bf16[32,2,12288]{2,1,0:T(2,128)(2,1)} %copy-done.1) | data formatting | bytes 3145728
  291.1 15.2 %copy.53 = bf16[32,16,6,256]{3,1,0,2:T(8,128)(2,1)} copy(bf16[32,16,6,256]{1,2,3,0:T(8,128)(2,1)} %bitcast.36) | data formatting | bytes 3145728 | tf_op jit(solution)/shard_map/all_to_all | solution.py:38
  306.3 0.3 convert_reduce_fusion.1
  306.6 21.9 %all-to-all-done.3 = bf16[8,512,512]{2,1,0:T(8,128)(2,1)} async-done(((bf16[8,512,512]{2,1,0:T(8,128)(2,1)}), bf16[8,512,512]{2,1,0:T(8,128)(2,1)}, u32[]{:S(2)}, u32[]{:S(2)}) %all-to-all-start.3) | async-done | bytes 4194336 | tf_op jit(solution)/shard_map/all_to_all | solution.py:31
  328.6 3.8 convert_reduce_fusion
  332.4 2.7 copy.54
  335.1 2.5 copy.55
  337.6 4.2 %convert_subtract_fusion = (f32[512,3,256]{2,0,1:T(8,128)}, f32[512,3,256]{2,0,1:T(8,128)}, f32[512,3,256]{2,0,1:T(8,128)}) fusion(bf16[16,3,32,256]{3,0,2,1:T(8,128)(2,1)S(1)} %copy.57, f32[512,1,256]{2,0,1:T(8,128)S(1)} %bitcast.47, f32[512,2,256]{2,0,1:T(8,128)} %copy.55, bf16[512,6,256]{2,0,1:T(8,128)(2,1)S(1)} %bitcast.43), kind=kLoop, calls=%fused_computation.13 | loop fusion | flops 7077888 | bytes 8650752 | tf_op jit(solution)/shard_map/sub | solution.py:65
  341.9 49.8 %reduce-scatter.2.cloned.1.call-done = bf16[16,4096]{1,0:T(8,128)(2,1)} async-done(((bf16[512,4096]{1,0:T(8,128)(2,1)}), bf16[16,4096]{1,0:T(8,128)(2,1)}) %reduce-scatter.2.cloned.1.call-update) | async-done | bytes 131088 | tf_op jit(solution)/shard_map/reduce_scatter | solution.py:108
  (21 shorter events, 0.1 us)
Async XLA Ops:
  7.2 2.9 copy-start.3
  7.2 190.1 %all-gather.2.cloned.1.call-start = ((), (), s32[]{:S(2)}) async-start(), calls=%async_computation.6 | async-start | bytes 8650752 | tf_op jit(solution)/shard_map/all_gather | solution.py:16
  93.6 5.4 %copy-start.6 = (f32[16,3,2560]{2,0,1:T(8,128)S(1)}, f32[16,3,2560]{2,0,1:T(8,128)}, u32[]{:S(2)}) copy-start(f32[16,3,2560]{2,0,1:T(8,128)} %param.16) | copy-start | bytes 1474564
  93.6 5.5 %copy-start.4 = (f32[16,3,5632]{2,0,1:T(8,128)S(1)}, f32[16,3,5632]{2,0,1:T(8,128)}, u32[]{:S(2)}) copy-start(f32[16,3,5632]{2,0,1:T(8,128)} %param.13) | copy-start | bytes 3244036
  93.6 88.9 %all-to-all-start.1 = ((bf16[8,512,3,256]{1,3,2,0:T(8,128)(2,1)}), bf16[8,512,3,256]{1,3,2,0:T(8,128)(2,1)}, u32[]{:S(2)}, u32[]{:S(2)}) async-start(bf16[8,512,3,256]{1,3,2,0:T(8,128)(2,1)} %stack.5), calls=%async_computation.1 | async-start | bytes 12582912 | tf_op jit(solution)/shard_map/all_to_all | solution.py:91
  99.0 1.0 copy-start.7
  99.0 1.4 copy-start.5
  132.5 55.9 %copy-start.8 = (f32[2560]{0:T(1024)S(1)}, f32[2560]{0:T(1024)}, u32[]{:S(2)}) copy-start(f32[2560]{0:T(1024)} %param.17) | copy-start | bytes 30724
  182.5 46.6 %all-to-all-start.2 = ((bf16[32,2,12288]{2,1,0:T(2,128)(2,1)}), bf16[32,2,12288]{2,1,0:T(2,128)(2,1)S(1)}, u32[]{:S(2)}, u32[]{:S(2)}) async-start(bf16[32,2,12288]{2,1,0:T(2,128)(2,1)} %reshape.34), calls=%async_computation.3 | async-start | bytes 3145728 | tf_op jit(solution)/shard_map/all_to_all | solution.py:38
  192.3 2.7 copy-start
  197.3 6.0 %copy-start.9 = (bf16[512,8192]{1,0:T(8,128)(2,1)S(1)}, bf16[512,8192]{1,0:T(8,128)(2,1)}, u32[]{:S(2)}) copy-start(bf16[512,8192]{1,0:T(8,128)(2,1)} %all-gather.2.cloned.1.call-done) | copy-start | bytes 25165828
  229.1 1.1 copy-start.1
  230.2 34.5 %all-to-all-start.4 = ((bf16[8,512,256]{2,1,0:T(8,128)(2,1)}), bf16[8,512,256]{2,1,0:T(8,128)(2,1)S(1)}, u32[]{:S(2)}, u32[]{:S(2)}) async-start(bf16[8,512,256]{2,1,0:T(8,128)(2,1)} %bitcast.48), calls=%async_computation.5 | async-start | bytes 4194304 | tf_op jit(solution)/shard_map/all_to_all | solution.py:31
  237.7 154.0 %reduce-scatter.2.cloned.1.call-start = ((), (), s32[]{:S(2)}) async-start(), calls=%async_computation.7 | async-start | bytes 4325376 | tf_op jit(solution)/shard_map/reduce_scatter | solution.py:108
  242.6 0.9 copy-start.10
  264.8 63.8 %all-to-all-start.3 = ((bf16[8,512,512]{2,1,0:T(8,128)(2,1)}), bf16[8,512,512]{2,1,0:T(8,128)(2,1)}, u32[]{:S(2)}, u32[]{:S(2)}) async-start(bf16[8,512,512]{2,1,0:T(8,128)(2,1)} %bitcast.44), calls=%async_computation.4 | async-start | bytes 8388608 | tf_op jit(solution)/shard_map/all_to_all | solution.py:31
  332.4 5.2 %copy-start.2 = (bf16[32,16,6,256]{3,1,0,2:T(8,128)(2,1)S(1)}, bf16[32,16,6,256]{3,1,0,2:T(8,128)(2,1)}, u32[]{:S(2)}) copy-start(bf16[32,16,6,256]{3,1,0,2:T(8,128)(2,1)} %copy.53) | copy-start | bytes 4718596
Sparse Core Ops, SparseCore 0:
  11.3 108.8 all-gather.1
  243.3 148.3 reduce-scatter.1
